TPU v7x, 32 devices: a whole 2x2x4 slice. The times are simulated.
32 devices in a mesh: layer: 2 (over y), latent: 8 (over z, x), tok: 2 (over core).
Axes of the slice: x: 2, y: 2, z: 4, core: 2. Of those that a mesh axis runs over, the one named last changes fastest.
Arguments:
- resid: bfloat16 [2, 384, 2304], P('layer', 'tok', 'latent'), may hold values from -6 to 6
- w_enc: bfloat16 [2, 2304, 2048], P('layer', None, 'latent'), may hold values from -0.09375 to 0.09375
- b_enc: float32 [2048], P('latent'), may hold values from -3 to 3
- w_dec: bfloat16 [2, 2048, 2304], P('layer', 'latent'), may hold values from -0.125 to 0.125
- b_dec: bfloat16 [2, 2304], P('layer', 'latent'), may hold values from -3 to 3
Outputs:
- grad_w_enc: bfloat16 [2, 2304, 2048], P('layer', 'tok', 'latent')
- grad_w_dec: bfloat16 [2, 2048, 2304], P('layer', 'latent')
All inputs are finite; a program needn't handle non-finite values.
Results may differ from a plain program's by a relative error of at most 0.023.
Values may be sent and summed in bfloat16 or wider, within the bound.
A program may use at most 64 MiB of HBM per device.

v0:
```python
import functools

import jax
import jax.numpy as jnp
from jax import lax
from jax.experimental import pallas as pl
from jax.experimental.pallas import tpu as pltpu
from jax.sharding import PartitionSpec as P

BETA = 4.0
LANES = 128
CHUNKS = 3
MESH = pl.DeviceIdType.MESH
F32 = jnp.float32
BF16 = jnp.bfloat16


def plain_shards(resid, w_enc, b_enc, w_dec, b_dec):
    decoder = w_dec[0]
    x_full = lax.all_gather(resid, "latent", axis=2, tiled=True)[0]
    bias_full = lax.all_gather(b_dec.reshape(1, 1, -1), "latent", axis=2, tiled=True)
    bias_full = bias_full.reshape(-1).astype(F32)
    tokens = x_full.shape[0] * lax.axis_size("tok")
    partial_value = jnp.dot(x_full, w_enc[0], preferred_element_type=F32)
    pre = lax.psum(partial_value.astype(BF16), "layer").astype(F32) + b_enc
    act = (jax.nn.softplus(BETA * pre) / BETA).astype(BF16)
    slope = jax.nn.sigmoid(BETA * pre)
    recon = lax.psum(
        jnp.dot(act, decoder, preferred_element_type=F32).astype(BF16), "latent"
    ).astype(F32)
    grad_all = (2.0 / tokens * (recon + bias_full - x_full.astype(F32))).astype(BF16)
    dec_sum = lax.dot_general(
        act, grad_all, (((0,), (0,)), ((), ())), preferred_element_type=F32
    )
    act_grad = lax.dot_general(
        grad_all, decoder, (((1,), (1,)), ((), ())), preferred_element_type=F32
    )
    grad_act = lax.psum(act_grad.astype(BF16), "layer").astype(F32)
    grad_pre = (grad_act * slope).astype(BF16)
    grad_w_dec = lax.psum(dec_sum.astype(BF16), "tok")
    grad_w_enc = lax.psum_scatter(
        lax.dot_general(
            x_full, grad_pre, (((0,), (0,)), ((), ())), preferred_element_type=F32
        ).astype(BF16),
        "tok",
        scatter_dimension=0,
        tiled=True,
    )
    return (grad_w_enc[None], grad_w_dec[None])


def kernel(
    n_lat, tokens,
    x_hbm, we_hbm, be_hbm, wd_hbm, bd_hbm,
    oe_ref, od_ref,
    x_ref, be_ref, bd_ref, we, wdv, wd, xb, xo, xt, gb, go, pre, slope, act, act_t, act_o, ys, yr, hs, hr, gp, gp_o,
    xs, xr, zs, cr, mine,
    load_sem, x_ss, x_rs, xo_rs, g_ss, g_rs, go_rs, one_ss, one_rs, xs_ss, xr_rs, zs_ss, cr_rs,
):
    rows, feats = x_ref.shape
    hid = we.shape[1]
    main = feats // LANES * LANES
    tiles = main // LANES
    rest = feats - main
    groups = LANES // rest
    sub = rows // groups
    nz = n_lat // 2
    half = n_lat // 2

    lay = lax.axis_index("layer")
    lat = lax.axis_index("latent")
    tok = lax.axis_index("tok")
    z, xx = lat // 2, lat % 2
    across = 2 * z + 1 - xx
    lay_o, tok_o = 1 - lay, 1 - tok

    loads = [
        pltpu.make_async_copy(src, dst, load_sem.at[i])
        for i, (src, dst) in enumerate(
            [(x_hbm, x_ref), (we_hbm, we), (wd_hbm, wdv), (be_hbm, be_ref), (bd_hbm, bd_ref)]
        )
    ]
    for load in loads:
        load.start()
    x_load, we_load, wd_load, be_load, bd_load = loads

    barrier = pltpu.get_barrier_semaphore()

    def greet(where):
        pl.semaphore_signal(barrier, inc=1, device_id=where, device_id_type=MESH)

    greet({"latent": across})
    greet({"layer": lay_o})
    greet({"tok": tok_o})

    @pl.when(z < nz - 1)
    def _():
        greet({"latent": lat + 2})

    @pl.when(z > 0)
    def _():
        greet({"latent": lat - 2})

    def remote(src, dst, ss, rs, where):
        return pltpu.make_async_remote_copy(
            src_ref=src, dst_ref=dst, send_sem=ss, recv_sem=rs,
            device_id=where, device_id_type=MESH,
        )

    lane = lax.broadcasted_iota(jnp.int32, (sub, LANES), 1) // rest

    def pack(full):
        out = jnp.zeros((sub, LANES), F32)
        for g in range(groups):
            out = jnp.where(lane == g, full[g * sub:(g + 1) * sub, main:], out)
        return jnp.concatenate(
            [full[:, i * LANES:(i + 1) * LANES] for i in range(tiles)] + [out], axis=0
        )

    def spread(block):
        packed = block[tiles * rows:]
        zero = jnp.zeros_like(packed)
        parts = jnp.concatenate(
            [jnp.where(lane == g, packed, zero) for g in range(groups)], axis=0
        )
        return jnp.concatenate(
            [block[i * rows:(i + 1) * rows] for i in range(tiles)] + [parts], axis=1
        )

    size = xb.shape[1]
    chunk = size // CHUNKS

    def part(ref, *at, c):
        return ref.at[(*at, pl.ds(c * chunk, chunk))]

    def if_up(fn):
        pl.when(z < nz - 1)(fn)

    def if_down(fn):
        pl.when(z > 0)(fn)

    def gather(buf, ss, rs, use, to_tok):
        def send(way, j, c):
            where = {"latent": (lat + 2, lat - 2, across)[way]}
            return remote(
                part(buf, j, c=c), part(buf, j, c=c), ss.at[way, j, c], rs.at[j, c], where
            )

        for c in range(CHUNKS):
            if_up(lambda: send(0, lat, c).start())
            if_down(lambda: send(1, lat, c).start())
            send(2, lat, c).start()
        to_tok(lat)
        use(lat)

        def side_block(j):
            for c in range(CHUNKS):
                send(2, j, c).wait_recv()
            to_tok(j)
            use(j)

        def far(s):
            pl.when(z - s >= 0)(lambda: side_block(across - 2 * s))
            pl.when(z + s < nz)(lambda: side_block(across + 2 * s))

        for s in range(1, nz):
            for c in range(CHUNKS):
                @pl.when(z - s >= 0)
                def _():
                    j = lat - 2 * s
                    send(2, j, c).wait_recv()
                    if_up(lambda: send(0, j, c).start())
                    send(2, j, c).start()

                @pl.when(z + s < nz)
                def _():
                    j = lat + 2 * s
                    send(2, j, c).wait_recv()
                    if_down(lambda: send(1, j, c).start())
                    send(2, j, c).start()

            @pl.when(z - s >= 0)
            def _():
                to_tok(lat - 2 * s)
                use(lat - 2 * s)

            @pl.when(z + s < nz)
            def _():
                to_tok(lat + 2 * s)
                use(lat + 2 * s)

            if s == 1:
                side_block(across)
            else:
                far(s - 1)
        far(nz - 1)

        def finish():
            for c in range(CHUNKS):
                send(2, lat, c).wait_send()
                if_up(lambda: send(0, lat, c).wait_send())
                if_down(lambda: send(1, lat, c).wait_send())
                for s in range(1, nz):
                    @pl.when(z - s >= 0)
                    def _():
                        send(2, lat - 2 * s, c).wait_send()
                        if_up(lambda: send(0, lat - 2 * s, c).wait_send())

                    @pl.when(z + s < nz)
                    def _():
                        send(2, lat + 2 * s, c).wait_send()
                        if_down(lambda: send(1, lat + 2 * s, c).wait_send())

        return finish

    x_load.wait()
    tail = x_ref[:, main:]
    wide = jnp.concatenate([x_ref[:, :main]] + [tail] * groups, axis=1)
    xb[lat] = pack(wide.astype(F32)).astype(BF16)
    pre[...] = jnp.zeros_like(pre)

    pl.semaphore_wait(barrier, 3 + (z + nz - 1) // nz + (2 * nz - 2 - z) // nz)

    def x_tok(i):
        return remote(
            xb.at[half * tok_o + i], xo.at[i], x_ss.at[3, i, 0], xo_rs.at[i], {"tok": tok_o}
        )

    def x_to_tok(j):
        @pl.when(j // half == tok_o)
        def _():
            x_tok(j - half * tok_o).start()

    def encode(j):
        lo = pl.multiple_of(j * feats, rest)
        w_main = we[pl.ds(lo, main), :]
        w_rest = we[pl.ds(pl.multiple_of(lo + main, rest), rest), :]
        w = jnp.concatenate([w_main] + [w_rest] * groups, axis=0)
        pre[...] += jnp.dot(spread(xb[j]), w, preferred_element_type=F32)

    we_load.wait()
    x_done = gather(xb, x_ss, x_rs, encode, x_to_tok)

    ys[...] = pre[...].astype(BF16)
    y_copy = remote(ys, yr, one_ss.at[0], one_rs.at[0], {"layer": lay_o})
    y_copy.start()
    wd_load.wait()
    for k in range(n_lat):
        lo = k * feats
        w_rest = wdv[:, lo + main:lo + feats]
        wd[k] = jnp.concatenate([wdv[:, lo:lo + main]] + [w_rest] * groups, axis=1)
    be_load.wait()
    bd_load.wait()
    y_copy.wait_recv()
    v = BETA * (pre[...] + yr[...].astype(F32) + be_ref[...])
    e = jnp.exp(-jnp.abs(v))
    act[...] = ((jnp.maximum(v, 0.0) + jnp.log1p(e)) / BETA).astype(BF16)
    slope[...] = jnp.where(v >= 0, 1.0, e) / (1.0 + e)

    order = [sign * d for d in range(nz - 1, 0, -1) for sign in (1, -1)]

    def each(fn):
        for d in order:
            pl.when(jnp.logical_and(z + d >= 0, z + d < nz))(functools.partial(fn, d))

    def x_send(zt, c):
        return remote(
            part(xs, zt, c=c), part(xr, zt, c=c), xs_ss.at[zt, c], xr_rs.at[zt, c],
            {"latent": across},
        )

    def z_send(way, zt, c):
        where = {"latent": (lat + 2, lat - 2)[way]}
        return remote(
            part(zs, zt, c=c), part(cr, way, zt, c=c), zs_ss.at[zt, c], cr_rs.at[way, zt, c], where
        )

    def decode(j):
        return pack(jnp.dot(act[...], wd[j], preferred_element_type=F32))

    def x_out(d):
        zt = z + d
        xs[zt] = decode(2 * zt + 1 - xx).astype(BF16)
        for c in range(CHUNKS):
            x_send(zt, c).start()

    def z_out(d):
        zt, way = z + d, (0 if d > 0 else 1)
        mine[...] = decode(2 * zt + xx)
        for c in range(CHUNKS):
            lo = pl.ds(c * chunk, chunk)
            x_send(zt, c).wait_recv()
            mine[lo] += xr[zt, lo].astype(F32)

            @pl.when(z > 0 if d > 0 else z < nz - 1)
            def _():
                z_send(way, zt, c).wait_recv()
                mine[lo] += cr[way, zt, lo].astype(F32)

            zs[zt, lo] = mine[lo].astype(BF16)
            z_send(way, zt, c).start()

    each(x_out)
    x_out(0)
    a_copy = remote(act, act_o, one_ss.at[1], one_rs.at[1], {"tok": tok_o})
    a_copy.start()
    each(z_out)
    total = decode(lat)
    bias = bd_ref[...].astype(F32)
    bias = jnp.concatenate([bias[:, :main]] + [bias[:, main:]] * groups, axis=1)
    total += jnp.concatenate(
        [jnp.broadcast_to(bias[:, i * LANES:(i + 1) * LANES], (rows, LANES)) for i in range(tiles)]
        + [jnp.broadcast_to(bias[:, main:], (sub, LANES))],
        axis=0,
    ) - xb[lat].astype(F32)
    for i in range(half):
        x_tok(i).wait_recv()
        both = jnp.concatenate([spread(xb[half * tok + i]), spread(xo[i])], axis=0)
        xt[i] = both.T
    a_copy.wait_recv()
    act_t[...] = jnp.concatenate([act[...], act_o[...]], axis=0).T
    mine[...] = total
    for c in range(CHUNKS):
        x_send(z, c).wait_recv()
    mine[...] += xr[z].astype(F32)

    def last(way):
        for c in range(CHUNKS):
            z_send(way, z, c).wait_recv()
        mine[...] += cr[way, z].astype(F32)

    if_down(lambda: last(0))
    if_up(lambda: last(1))
    total = mine[...]
    gb[lat] = (2.0 / tokens * total).astype(BF16)
    pre[...] = jnp.zeros_like(pre)

    def g_tok(j):
        return remote(gb.at[j], go.at[j], g_ss.at[3, j, 0], go_rs.at[j], {"tok": tok_o})

    def g_to_tok(j):
        g_tok(j).start()

    def back(j):
        pre[...] += lax.dot_general(
            spread(gb[j]), wd[j], (((1,), (1,)), ((), ())), preferred_element_type=F32
        )

    g_done = gather(gb, g_ss, g_rs, back, g_to_tok)

    hs[...] = pre[...].astype(BF16)
    h_copy = remote(hs, hr, one_ss.at[2], one_rs.at[2], {"layer": lay_o})
    h_copy.start()

    row = []
    for j in range(n_lat):
        g_tok(j).wait_recv()
        both = jnp.concatenate([spread(gb[j]), spread(go[j])], axis=0)
        dw = jnp.dot(act_t[...], both, preferred_element_type=F32)
        r = dw[:, main:main + rest]
        for g in range(1, groups):
            r = r + dw[:, main + g * rest:main + (g + 1) * rest]
        row += [dw[:, :main], r]
        if (j + 1) * feats % LANES == 0:
            width = sum(p.shape[1] for p in row)
            od_ref[:, (j + 1) * feats - width:(j + 1) * feats] = jnp.concatenate(
                row, axis=1
            ).astype(BF16)
            row = []

    h_copy.wait_recv()
    gp[...] = ((pre[...] + hr[...].astype(F32)) * slope[...]).astype(BF16)
    p_copy = remote(gp, gp_o, one_ss.at[3], one_rs.at[3], {"tok": tok_o})
    p_copy.start()
    p_copy.wait_recv()
    gp_both = jnp.concatenate([gp[...], gp_o[...]], axis=0)
    for i in range(half):
        dw = jnp.dot(xt[i], gp_both, preferred_element_type=F32)
        r = dw[main:main + rest]
        for g in range(1, groups):
            r = r + dw[main + g * rest:main + (g + 1) * rest]
        oe_ref[i * feats:(i + 1) * feats] = jnp.concatenate([dw[:main], r], axis=0).astype(BF16)

    x_done()
    g_done()
    for i in range(half):
        x_tok(i).wait_send()
    for j in range(n_lat):
        g_tok(j).wait_send()
    y_copy.wait_send()
    a_copy.wait_send()
    h_copy.wait_send()
    p_copy.wait_send()
    for c in range(CHUNKS):
        each(lambda d: x_send(z + d, c).wait_send())
        x_send(z, c).wait_send()
        each(lambda d: z_send(0 if d > 0 else 1, z + d, c).wait_send())


def fused_shards(n_lat, resid, w_enc, b_enc, w_dec, b_dec):
    x, we, wd = resid[0], w_enc[0], w_dec[0]
    rows, feats = x.shape
    total, hid = we.shape
    main = feats // LANES * LANES
    wide = main + LANES
    block = rows * feats // LANES
    half, nz = n_lat // 2, n_lat // 2
    dma = pltpu.SemaphoreType.DMA
    vm = pltpu.VMEM
    blocks = vm((n_lat, block, LANES), BF16)
    blocks_z = vm((nz, block, LANES), BF16)
    square = vm((rows, hid), BF16)
    in_vmem = pl.BlockSpec(memory_space=pltpu.VMEM)
    in_hbm = pl.BlockSpec(memory_space=pltpu.HBM)
    ge, gd = pl.pallas_call(
        functools.partial(kernel, n_lat, rows * 2),
        out_shape=(
            jax.ShapeDtypeStruct((half * feats, hid), BF16),
            jax.ShapeDtypeStruct((hid, total), BF16),
        ),
        in_specs=[in_hbm] * 5,
        out_specs=(in_vmem, in_vmem),
        scratch_shapes=[
            vm((rows, feats), BF16), vm((1, hid), F32), vm((1, feats), BF16),
            vm((total, hid), BF16),
            vm((hid, total), BF16),
            vm((n_lat, hid, wide), BF16),
            blocks,
            vm((half, block, LANES), BF16),
            vm((half, wide, 2 * rows), BF16),
            blocks, blocks,
            vm((rows, hid), F32), vm((rows, hid), F32),
            square, vm((hid, 2 * rows), BF16), square,
            square, square, square, square, square, square,
            blocks_z, blocks_z, blocks_z, vm((2, nz, block, LANES), BF16),
            vm((block, LANES), F32),
            dma((5,)),
            dma((4, n_lat, CHUNKS)), dma((n_lat, CHUNKS)), dma((half,)),
            dma((4, n_lat, CHUNKS)), dma((n_lat, CHUNKS)), dma((n_lat,)),
            dma((4,)), dma((4,)),
            dma((nz, CHUNKS)), dma((nz, CHUNKS)), dma((nz, CHUNKS)), dma((2, nz, CHUNKS)),
        ],
        compiler_params=pltpu.CompilerParams(
            collective_id=0, has_side_effects=True, vmem_limit_bytes=48 * 2**20
        ),
    )(*(
        pltpu.with_memory_space_constraint(v, pltpu.HBM)
        for v in (x, we, b_enc.reshape(1, -1), wd, b_dec)
    ))
    return ge[None], gd[None]


def packs(mesh, rows, feats):
    rest = feats % LANES
    if mesh.shape["layer"] != 2 or mesh.shape["tok"] != 2 or mesh.shape["latent"] % 4:
        return False
    if rest == 0 or rest % 32 or LANES % rest:
        return False
    fits = rows % (16 * (LANES // rest)) == 0 and feats > LANES
    return fits and rows * feats // LANES % (8 * CHUNKS) == 0


def solution(mesh):
    def shards(resid, w_enc, b_enc, w_dec, b_dec):
        _, rows, feats = resid.shape
        if packs(mesh, rows, feats) and resid.shape[0] == 1:
            return fused_shards(mesh.shape["latent"], resid, w_enc, b_enc, w_dec, b_dec)
        return plain_shards(resid, w_enc, b_enc, w_dec, b_dec)

    placed = (
        P("layer", "tok", "latent"),
        P("layer", None, "latent"),
        P("latent"),
        P("layer", "latent", None),
        P("layer", "latent"),
    )
    return jax.shard_map(
        shards,
        mesh=mesh,
        in_specs=placed,
        out_specs=(P("layer", "tok", "latent"), P("layer", "latent", None)),
        check_vma=False,
    )
```

profile of v0, /device:TPU:0, one launch (start us, length us, event | category | flops | bytes accessed | tf_op | source)
XLA Modules:
  0.0 60.5 jit_solution(11458329759563833584)
XLA Ops:
  0.6 58.0 %shard_map.68 = (bf16[1152,256]{1,0:T(8,128)(2,1)S(1)}, bf16[256,2304]{1,0:T(8,128)(2,1)S(1)}) custom-call(bf16[192,288]{1,0:T(8,128)(2,1)} %bitcast.10, bf16[2304,256]{1,0:T(8,128)(2,1)} %bitcast.8, f32[1,256]{1,0:T(1,128)} %bitcast.11, bf16[256,2304]{1,0:T(8,128)(2,1)} %bitcast.9, bf16[1,288]{1,0:T(2,128)(2,1)} %bd_hbm.1), custom_call_target="tpu_custom_call" | custom-call | tf_op jit(solution)/shard_map/pallas_call | solution.py:415
  58.7 0.8 %copy.9 = bf16[1,1152,256]{2,1,0:T(8,128)(2,1)} copy(bf16[1,1152,256]{2,1,0:T(8,128)(2,1)S(1)} %bitcast.7) | data formatting | bytes 1179648
  59.5 1.0 %copy.10 = bf16[1,256,2304]{2,1,0:T(8,128)(2,1)} copy(bf16[1,256,2304]{2,1,0:T(8,128)(2,1)S(1)} %bitcast.6) | data formatting | bytes 2359296
where the time goes:
time: 61.3 us; the launch traced here: 60.5 us
  Pallas kernels  58 us (95%)
  local copies, waits for them, and re-layouts  1.83 us (3%)
  between operations  0.64 us (1%)
    pallas_call x1, Pallas kernels, fused_shards(): pl.pallas_call(functools.partial(kernel, n_lat, rows * 2), out_shape=(jax...  58 us
    unnamed x2, local copies, waits for them, and re-layouts  1.83 us

commit v1 on v0

v1 whole, which is shorter than its diff:
```python
import functools

import jax
import jax.numpy as jnp
from jax import lax
from jax.experimental import pallas as pl
from jax.experimental.pallas import tpu as pltpu
from jax.sharding import PartitionSpec as P

BETA = 4.0
LANES = 128
CHUNKS = 3
MESH = pl.DeviceIdType.MESH
F32 = jnp.float32
BF16 = jnp.bfloat16


def plain_shards(resid, w_enc, b_enc, w_dec, b_dec):
    decoder = w_dec[0]
    x_full = lax.all_gather(resid, "latent", axis=2, tiled=True)[0]
    bias_full = lax.all_gather(b_dec.reshape(1, 1, -1), "latent", axis=2, tiled=True)
    bias_full = bias_full.reshape(-1).astype(F32)
    tokens = x_full.shape[0] * lax.axis_size("tok")
    partial_value = jnp.dot(x_full, w_enc[0], preferred_element_type=F32)
    pre = lax.psum(partial_value.astype(BF16), "layer").astype(F32) + b_enc
    act = (jax.nn.softplus(BETA * pre) / BETA).astype(BF16)
    slope = jax.nn.sigmoid(BETA * pre)
    recon = lax.psum(
        jnp.dot(act, decoder, preferred_element_type=F32).astype(BF16), "latent"
    ).astype(F32)
    grad_all = (2.0 / tokens * (recon + bias_full - x_full.astype(F32))).astype(BF16)
    dec_sum = lax.dot_general(
        act, grad_all, (((0,), (0,)), ((), ())), preferred_element_type=F32
    )
    act_grad = lax.dot_general(
        grad_all, decoder, (((1,), (1,)), ((), ())), preferred_element_type=F32
    )
    grad_act = lax.psum(act_grad.astype(BF16), "layer").astype(F32)
    grad_pre = (grad_act * slope).astype(BF16)
    grad_w_dec = lax.psum(dec_sum.astype(BF16), "tok")
    grad_w_enc = lax.psum_scatter(
        lax.dot_general(
            x_full, grad_pre, (((0,), (0,)), ((), ())), preferred_element_type=F32
        ).astype(BF16),
        "tok",
        scatter_dimension=0,
        tiled=True,
    )
    return (grad_w_enc[None], grad_w_dec[None])


def kernel(
    n_lat, tokens,
    x_hbm, we_hbm, be_hbm, wd_hbm, bd_hbm,
    oe_ref, od_ref,
    x_ref, be_ref, bd_ref, we, wdv, wd, xb, xo, xt, gb, go, pre, slope, act, act_t, act_o, ys, yr, hs, hr, gp, gp_o,
    xs, xr, zs, cr, bias_x,
    load_sem, we_sem, x_ss, x_rs, xo_ss, xo_rs, g_ss, g_rs, go_ss, go_rs, one_ss, one_rs, xs_ss, xr_rs, zs_ss, cr_rs,
):
    rows, feats = x_ref.shape
    hid = we.shape[2]
    main = feats // LANES * LANES
    tiles = main // LANES
    rest = feats - main
    groups = LANES // rest
    part = rows // CHUNKS
    sub = part // groups
    nz = n_lat // 2
    half = n_lat // 2

    lay = lax.axis_index("layer")
    lat = lax.axis_index("latent")
    tok = lax.axis_index("tok")
    z, xx = lat // 2, lat % 2
    across = {"latent": 2 * z + 1 - xx}
    other_layer = {"layer": 1 - lay}
    tok_o = 1 - tok
    other_tok = {"tok": tok_o}
    inner = jnp.logical_and(z > 0, z < nz - 1)

    def peer(k):
        if k == 0:
            return z
        if k == 1:
            return z + 1 - 2 * (z % 2)
        if k == 2:
            return (z + 2) % 4
        return nz - 1 - z

    def same(k):
        return 2 * peer(k) + xx

    def cross(k):
        return 2 * peer(k) + 1 - xx

    loads = [
        pltpu.make_async_copy(src, dst, load_sem.at[i])
        for i, (src, dst) in enumerate(
            [(x_hbm, x_ref), (wd_hbm, wdv), (be_hbm, be_ref), (bd_hbm, bd_ref)]
        )
    ]
    we_loads = []
    for j in range(n_lat):
        lo = j * feats
        we_loads.append(pltpu.make_async_copy(
            we_hbm.at[pl.ds(lo, main)], we.at[j, pl.ds(0, main)], we_sem.at[j, 0]
        ))
        for g in range(groups):
            we_loads.append(pltpu.make_async_copy(
                we_hbm.at[pl.ds(lo + main, rest)], we.at[j, pl.ds(main + g * rest, rest)],
                we_sem.at[j, 1 + g],
            ))
    loads[0].start()
    x_load, wd_load, be_load, bd_load = loads

    barrier = pltpu.get_barrier_semaphore()

    def greet(where):
        pl.semaphore_signal(barrier, inc=1, device_id=where, device_id_type=MESH)

    for k in range(1, nz):
        greet({"latent": same(k)})
    greet(across)
    greet(other_layer)
    greet(other_tok)
    for load in loads[1:] + we_loads:
        load.start()

    def remote(src, dst, ss, rs, where):
        return pltpu.make_async_remote_copy(
            src_ref=src, dst_ref=dst, send_sem=ss, recv_sem=rs,
            device_id=where, device_id_type=MESH,
        )

    lane = lax.broadcasted_iota(jnp.int32, (sub, LANES), 1) // rest

    def pack(full):
        out = jnp.zeros((sub, LANES), F32)
        for g in range(groups):
            out = jnp.where(lane == g, full[g * sub:(g + 1) * sub, main:], out)
        return jnp.concatenate(
            [full[:, i * LANES:(i + 1) * LANES] for i in range(tiles)] + [out], axis=0
        )

    def spread(block):
        packed = block[tiles * part:]
        zero = jnp.zeros_like(packed)
        parts = jnp.concatenate(
            [jnp.where(lane == g, packed, zero) for g in range(groups)], axis=0
        )
        return jnp.concatenate(
            [block[i * part:(i + 1) * part] for i in range(tiles)] + [parts], axis=1
        )

    def spread_all(ref, j):
        return [spread(ref[c, j]) for c in range(CHUNKS)]

    def gather(buf, ss, rs):
        def send(way, c, j):
            where = across if way == 0 else {"latent": same(way)}
            return remote(buf.at[c, j], buf.at[c, j], ss.at[way, c, j], rs.at[c, j], where)

        def own(c):
            send(0, c, lat).start()
            send(1, c, lat).start()
            pl.when(inner)(lambda: send(3, c, lat).start())
            send(2, c, lat).start()

        def relay(c, k):
            j = same(k)
            send(0, c, j).wait_recv()
            send(0, c, j).start()
            if k == 2:
                pl.when(inner)(lambda: send(1, c, j).start())

        def arrive(c, k):
            send(0, c, cross(k)).wait_recv()

        def finish():
            for c in range(CHUNKS):
                for k in range(nz):
                    send(0, c, same(k)).wait_send()
                send(1, c, lat).wait_send()
                send(2, c, lat).wait_send()

                @pl.when(inner)
                def _():
                    send(3, c, lat).wait_send()
                    send(1, c, same(2)).wait_send()

        return own, relay, arrive, finish

    x_own, x_relay, x_arrive, x_finish = gather(xb, x_ss, x_rs)
    g_own, g_relay, g_arrive, g_finish = gather(gb, g_ss, g_rs)

    def x_tok(i):
        return remote(
            xb.at[:, half * tok_o + i], xo.at[:, i], xo_ss.at[i], xo_rs.at[i], other_tok
        )

    def g_tok(c):
        return remote(gb.at[c], go.at[c], go_ss.at[c], go_rs.at[c], other_tok)

    def one(i, src, dst, c, where):
        return remote(src.at[c], dst.at[c], one_ss.at[i, c], one_rs.at[i, c], where)

    def y_copy(c):
        return one(0, ys, yr, c, other_layer)

    def a_copy(c):
        return one(1, act, act_o, c, other_tok)

    def h_copy(c):
        return one(2, hs, hr, c, other_layer)

    def p_copy(c):
        return one(3, gp, gp_o, c, other_tok)

    def x_send(c, k):
        return remote(xs.at[c, k], xr.at[c, k], xs_ss.at[c, k], xr_rs.at[c, k], across)

    def z_send(c, k):
        return remote(
            zs.at[c, k], cr.at[c, k], zs_ss.at[c, k], cr_rs.at[c, k], {"latent": same(k)}
        )

    def encode(c, j):
        pre[c] += jnp.dot(spread(xb[c, j]), we[j], preferred_element_type=F32)

    def y_out(c):
        ys[c] = pre[c].astype(BF16)
        y_copy(c).start()

    def activate(c):
        y_copy(c).wait_recv()
        v = BETA * (pre[c] + yr[c].astype(F32) + be_ref[...])
        e = jnp.exp(-jnp.abs(v))
        act[c] = ((jnp.maximum(v, 0.0) + jnp.log1p(e)) / BETA).astype(BF16)
        slope[c] = jnp.where(v >= 0, 1.0, e) / (1.0 + e)
        a_copy(c).start()

    def decode(c, j):
        return pack(jnp.dot(act[c], wd[j], preferred_element_type=F32))

    def x_out(c, k):
        xs[c, k] = decode(c, cross(k)).astype(BF16)
        x_send(c, k).start()

    def z_out(c, k):
        mine = decode(c, same(k))
        x_send(c, k).wait_recv()
        zs[c, k] = (mine + xr[c, k].astype(F32)).astype(BF16)
        z_send(c, k).start()

    def settle(c):
        total = decode(c, lat) + bias_x[c]
        x_send(c, 0).wait_recv()
        total += xr[c, 0].astype(F32)
        for k in range(1, nz):
            z_send(c, k).wait_recv()
            total += cr[c, k].astype(F32)
        gb[c, lat] = (2.0 / tokens * total).astype(BF16)
        g_own(c)

    def back(c, j):
        d = lax.dot_general(
            spread(gb[c, j]), wd[j], (((1,), (1,)), ((), ())), preferred_element_type=F32
        )
        pre[c] += d

    def back_first(c):
        pre[c] = lax.dot_general(
            spread(gb[c, lat]), wd[lat], (((1,), (1,)), ((), ())), preferred_element_type=F32
        )

    def h_out(c):
        hs[c] = pre[c].astype(BF16)
        h_copy(c).start()
        g_tok(c).start()

    def grad_pre(c):
        h_copy(c).wait_recv()
        gp[c] = ((pre[c] + hr[c].astype(F32)) * slope[c]).astype(BF16)
        p_copy(c).start()

    def both(own, other, j_own, j_other):
        return jnp.concatenate(spread_all(own, j_own) + spread_all(other, j_other), axis=0)

    def turn_x():
        for i in range(half):
            x_tok(i).wait_recv()
            xt[i] = both(xb, xo, half * tok + i, i).T

    def turn_act():
        for c in range(CHUNKS):
            a_copy(c).wait_recv()
        act_t[...] = jnp.concatenate(
            [act[c] for c in range(CHUNKS)] + [act_o[c] for c in range(CHUNKS)], axis=0
        ).T

    def widen_decoder():
        wd_load.wait()
        for k in range(n_lat):
            lo = k * feats
            w_rest = wdv[:, lo + main:lo + feats]
            wd[k] = jnp.concatenate([wdv[:, lo:lo + main]] + [w_rest] * groups, axis=1)

    def fill_bias():
        bias = bd_ref[...].astype(F32)
        bias = jnp.concatenate([bias[:, :main]] + [bias[:, main:]] * groups, axis=1)
        block = jnp.concatenate(
            [jnp.broadcast_to(bias[:, i * LANES:(i + 1) * LANES], (part, LANES)) for i in range(tiles)]
            + [jnp.broadcast_to(bias[:, main:], (sub, LANES))],
            axis=0,
        )
        for c in range(CHUNKS):
            bias_x[c] = block - xb[c, lat].astype(F32)

    x_load.wait()
    tail = x_ref[:, main:]
    wide = jnp.concatenate([x_ref[:, :main]] + [tail] * groups, axis=1).astype(F32)
    for c in range(CHUNKS):
        xb[c, lat] = pack(wide[c * part:(c + 1) * part]).astype(BF16)

    pl.semaphore_wait(barrier, nz + 2)
    for c in range(CHUNKS):
        x_own(c)
    for load in we_loads:
        load.wait()
    be_load.wait()
    bd_load.wait()
    for c in range(CHUNKS):
        pre[c] = jnp.dot(spread(xb[c, lat]), we[lat], preferred_element_type=F32)
    widen_decoder()
    fill_bias()

    def relay_encode(c):
        for k in range(1, nz):
            x_relay(c, k)
        for k in range(1, nz):
            encode(c, same(k))

    def arrive_encode(c):
        for k in range(nz):
            x_arrive(c, k)
            encode(c, cross(k))

    relay_encode(0)
    relay_encode(1)
    arrive_encode(0)
    y_out(0)
    relay_encode(2)
    arrive_encode(1)
    y_out(1)
    activate(0)
    for k in (3, 2, 1, 0):
        x_out(0, k)
    arrive_encode(2)
    y_out(2)
    for i in range(half):
        x_tok(i).start()
    activate(1)
    for k in (3, 2, 1, 0):
        x_out(1, k)
    for k in (3, 2, 1):
        z_out(0, k)
    activate(2)
    for k in (3, 2, 1, 0):
        x_out(2, k)
    for k in (3, 2, 1):
        z_out(1, k)
    turn_x()
    settle(0)
    for k in (3, 2, 1):
        z_out(2, k)
    turn_act()
    settle(1)
    back_first(0)

    def relay_back(c):
        for k in range(1, nz):
            g_relay(c, k)
        for k in range(1, nz):
            back(c, same(k))

    def arrive_back(c):
        for k in range(nz):
            g_arrive(c, k)
            back(c, cross(k))

    relay_back(0)
    settle(2)
    back_first(1)
    back_first(2)
    relay_back(1)
    arrive_back(0)
    h_out(0)
    relay_back(2)
    arrive_back(1)
    h_out(1)
    grad_pre(0)
    arrive_back(2)
    h_out(2)
    grad_pre(1)
    for c in range(CHUNKS):
        g_tok(c).wait_recv()

    row = []
    for j in range(n_lat):
        dw = jnp.dot(act_t[...], both(gb, go, j, j), preferred_element_type=F32)
        r = dw[:, main:main + rest]
        for g in range(1, groups):
            r = r + dw[:, main + g * rest:main + (g + 1) * rest]
        row += [dw[:, :main], r]
        if (j + 1) * feats % LANES == 0:
            width = sum(p.shape[1] for p in row)
            od_ref[:, (j + 1) * feats - width:(j + 1) * feats] = jnp.concatenate(
                row, axis=1
            ).astype(BF16)
            row = []

    grad_pre(2)
    for c in range(CHUNKS):
        p_copy(c).wait_recv()
    gp_both = jnp.concatenate(
        [gp[c] for c in range(CHUNKS)] + [gp_o[c] for c in range(CHUNKS)], axis=0
    )
    for i in range(half):
        dw = jnp.dot(xt[i], gp_both, preferred_element_type=F32)
        r = dw[main:main + rest]
        for g in range(1, groups):
            r = r + dw[main + g * rest:main + (g + 1) * rest]
        oe_ref[i * feats:(i + 1) * feats] = jnp.concatenate([dw[:main], r], axis=0).astype(BF16)

    x_finish()
    g_finish()
    for i in range(half):
        x_tok(i).wait_send()
    for c in range(CHUNKS):
        for copy in (g_tok, y_copy, a_copy, h_copy, p_copy):
            copy(c).wait_send()
        x_send(c, 0).wait_send()
        for k in range(1, nz):
            x_send(c, k).wait_send()
            z_send(c, k).wait_send()


def fused_shards(n_lat, resid, w_enc, b_enc, w_dec, b_dec):
    x, we, wd = resid[0], w_enc[0], w_dec[0]
    rows, feats = x.shape
    total, hid = we.shape
    main = feats // LANES * LANES
    wide = main + LANES
    groups = LANES // (feats - main)
    part = rows // CHUNKS
    block = part * feats // LANES
    half, nz = n_lat // 2, n_lat // 2
    dma = pltpu.SemaphoreType.DMA
    vm = pltpu.VMEM
    blocks = vm((CHUNKS, n_lat, block, LANES), BF16)
    blocks_z = vm((CHUNKS, nz, block, LANES), BF16)
    square = vm((CHUNKS, part, hid), BF16)
    square_f = vm((CHUNKS, part, hid), F32)
    in_vmem = pl.BlockSpec(memory_space=pltpu.VMEM)
    in_hbm = pl.BlockSpec(memory_space=pltpu.HBM)
    ge, gd = pl.pallas_call(
        functools.partial(kernel, n_lat, rows * 2),
        out_shape=(
            jax.ShapeDtypeStruct((half * feats, hid), BF16),
            jax.ShapeDtypeStruct((hid, total), BF16),
        ),
        in_specs=[in_hbm] * 5,
        out_specs=(in_vmem, in_vmem),
        scratch_shapes=[
            vm((rows, feats), BF16), vm((1, hid), F32), vm((1, feats), BF16),
            vm((n_lat, wide, hid), BF16),
            vm((hid, total), BF16),
            vm((n_lat, hid, wide), BF16),
            blocks,
            vm((CHUNKS, half, block, LANES), BF16),
            vm((half, wide, 2 * rows), BF16),
            blocks, blocks,
            square_f, square_f,
            square, vm((hid, 2 * rows), BF16), square,
            square, square, square, square, square, square,
            blocks_z, blocks_z, blocks_z, blocks_z,
            vm((CHUNKS, block, LANES), F32),
            dma((4,)), dma((n_lat, 1 + groups)),
            dma((4, CHUNKS, n_lat)), dma((CHUNKS, n_lat)), dma((half,)), dma((half,)),
            dma((4, CHUNKS, n_lat)), dma((CHUNKS, n_lat)), dma((CHUNKS,)), dma((CHUNKS,)),
            dma((4, CHUNKS)), dma((4, CHUNKS)),
            dma((CHUNKS, nz)), dma((CHUNKS, nz)), dma((CHUNKS, nz)), dma((CHUNKS, nz)),
        ],
        compiler_params=pltpu.CompilerParams(
            collective_id=0, has_side_effects=True, vmem_limit_bytes=48 * 2**20
        ),
    )(*(
        pltpu.with_memory_space_constraint(v, pltpu.HBM)
        for v in (x, we, b_enc.reshape(1, -1), wd, b_dec)
    ))
    return ge[None], gd[None]


def packs(mesh, rows, feats):
    rest = feats % LANES
    if mesh.shape["layer"] != 2 or mesh.shape["tok"] != 2 or mesh.shape["latent"] != 8:
        return False
    if rest == 0 or rest % 32 or LANES % rest:
        return False
    return rows % (16 * CHUNKS * (LANES // rest)) == 0 and feats > LANES


def solution(mesh):
    def shards(resid, w_enc, b_enc, w_dec, b_dec):
        _, rows, feats = resid.shape
        if packs(mesh, rows, feats) and resid.shape[0] == 1:
            return fused_shards(mesh.shape["latent"], resid, w_enc, b_enc, w_dec, b_dec)
        return plain_shards(resid, w_enc, b_enc, w_dec, b_dec)

    placed = (
        P("layer", "tok", "latent"),
        P("layer", None, "latent"),
        P("latent"),
        P("layer", "latent", None),
        P("layer", "latent"),
    )
    return jax.shard_map(
        shards,
        mesh=mesh,
        in_specs=placed,
        out_specs=(P("layer", "tok", "latent"), P("layer", "latent", None)),
        check_vma=False,
    )
```

time: 61.3 us -> 57 us (0.930); the launches traced: 60.5 us -> 56.8 us
  Pallas kernels: 58 us -> 54.4 us
    pallas_call x1, Pallas kernels: 58 us -> 54.4 us  [fused_shards(): pl.pallas_call(functools.partial(kernel, n_lat, rows * 2), out_shape=(jax...]
where the time goes in v1:
time: 57 us; the launch traced here: 56.8 us
  Pallas kernels  54.4 us (95%)
  local copies, waits for them, and re-layouts  1.83 us (3%)
  between operations  0.64 us (1%)
    pallas_call x1, Pallas kernels, fused_shards(): pl.pallas_call(functools.partial(kernel, n_lat, rows * 2), out_shape=(jax...  54.4 us
    unnamed x2, local copies, waits for them, and re-layouts  1.83 us

profile of v1, /device:TPU:0, one launch (start us, length us, event | category | flops | bytes accessed | tf_op | source)
XLA Modules:
  0.0 56.8 jit_solution(6676786774899886426)
XLA Ops:
  0.6 54.4 %shard_map.68 = (bf16[1152,256]{1,0:T(8,128)(2,1)S(1)}, bf16[256,2304]{1,0:T(8,128)(2,1)S(1)}) custom-call(bf16[192,288]{1,0:T(8,128)(2,1)} %bitcast.10, bf16[2304,256]{1,0:T(8,128)(2,1)} %bitcast.8, f32[1,256]{1,0:T(1,128)} %bitcast.11, bf16[256,2304]{1,0:T(8,128)(2,1)} %bitcast.9, bf16[1,288]{1,0:T(2,128)(2,1)} %bd_hbm.1), custom_call_target="tpu_custom_call" | custom-call | tf_op jit(solution)/shard_map/pallas_call | solution.py:466
  55.0 0.8 %copy.9 = bf16[1,1152,256]{2,1,0:T(8,128)(2,1)} copy(bf16[1,1152,256]{2,1,0:T(8,128)(2,1)S(1)} %bitcast.7) | data formatting | bytes 1179648
  55.8 1.0 %copy.10 = bf16[1,256,2304]{2,1,0:T(8,128)(2,1)} copy(bf16[1,256,2304]{2,1,0:T(8,128)(2,1)S(1)} %bitcast.6) | data formatting | bytes 2359296

commit v2 on v1

--- a/solution.py
+++ b/solution.py
@@ -52,8 +52,8 @@
 def kernel(
     n_lat, tokens,
     x_hbm, we_hbm, be_hbm, wd_hbm, bd_hbm,
-    oe_ref, od_ref,
-    x_ref, be_ref, bd_ref, we, wdv, wd, xb, xo, xt, gb, go, pre, slope, act, act_t, act_o, ys, yr, hs, hr, gp, gp_o,
+    gp_both, xt, od_ref,
+    x_ref, be_ref, bd_ref, we, wdv, wd, xb, xo, gb, go, pre, slope, act, act_t, act_o, ys, yr, hs, hr, gp, gp_o,
     xs, xr, zs, cr, bias_x,
     load_sem, we_sem, x_ss, x_rs, xo_ss, xo_rs, g_ss, g_rs, go_ss, go_rs, one_ss, one_rs, xs_ss, xr_rs, zs_ss, cr_rs,
 ):
@@ -422,15 +422,10 @@
     grad_pre(2)
     for c in range(CHUNKS):
         p_copy(c).wait_recv()
-    gp_both = jnp.concatenate(
-        [gp[c] for c in range(CHUNKS)] + [gp_o[c] for c in range(CHUNKS)], axis=0
-    )
-    for i in range(half):
-        dw = jnp.dot(xt[i], gp_both, preferred_element_type=F32)
-        r = dw[main:main + rest]
-        for g in range(1, groups):
-            r = r + dw[main + g * rest:main + (g + 1) * rest]
-        oe_ref[i * feats:(i + 1) * feats] = jnp.concatenate([dw[:main], r], axis=0).astype(BF16)
+    half_rows = CHUNKS * part
+    for c in range(CHUNKS):
+        gp_both[c * part:(c + 1) * part] = gp[c]
+        gp_both[half_rows + c * part:half_rows + (c + 1) * part] = gp_o[c]
 
     x_finish()
     g_finish()
@@ -443,6 +438,28 @@
         for k in range(1, nz):
             x_send(c, k).wait_send()
             z_send(c, k).wait_send()
+
+
+def finish_kernel(gp_ref, xt_ref, dec_ref, oe_hbm, od_hbm, oe, sem, dec_sem):
+    half, wide, _ = xt_ref.shape
+    main = wide - LANES
+    feats = oe.shape[1]
+    rest = feats - main
+    dec = pltpu.make_async_copy(dec_ref, od_hbm, dec_sem)
+    dec.start()
+    copies = []
+    for i in range(half):
+        dw = jnp.dot(xt_ref[i], gp_ref[...], preferred_element_type=F32)
+        r = dw[main:main + rest]
+        for g in range(1, LANES // rest):
+            r = r + dw[main + g * rest:main + (g + 1) * rest]
+        oe[i] = jnp.concatenate([dw[:main], r], axis=0).astype(BF16)
+        copy = pltpu.make_async_copy(oe.at[i], oe_hbm.at[pl.ds(i * feats, feats)], sem.at[i])
+        copy.start()
+        copies.append(copy)
+    for copy in copies:
+        copy.wait()
+    dec.wait()
 
 
 def fused_shards(n_lat, resid, w_enc, b_enc, w_dec, b_dec):
@@ -463,14 +480,15 @@
     square_f = vm((CHUNKS, part, hid), F32)
     in_vmem = pl.BlockSpec(memory_space=pltpu.VMEM)
     in_hbm = pl.BlockSpec(memory_space=pltpu.HBM)
-    ge, gd = pl.pallas_call(
+    gp_both, xt, dec = pl.pallas_call(
         functools.partial(kernel, n_lat, rows * 2),
         out_shape=(
-            jax.ShapeDtypeStruct((half * feats, hid), BF16),
+            jax.ShapeDtypeStruct((2 * rows, hid), BF16),
+            jax.ShapeDtypeStruct((half, wide, 2 * rows), BF16),
             jax.ShapeDtypeStruct((hid, total), BF16),
         ),
         in_specs=[in_hbm] * 5,
-        out_specs=(in_vmem, in_vmem),
+        out_specs=(in_vmem,) * 3,
         scratch_shapes=[
             vm((rows, feats), BF16), vm((1, hid), F32), vm((1, feats), BF16),
             vm((n_lat, wide, hid), BF16),
@@ -478,7 +496,6 @@
             vm((n_lat, hid, wide), BF16),
             blocks,
             vm((CHUNKS, half, block, LANES), BF16),
-            vm((half, wide, 2 * rows), BF16),
             blocks, blocks,
             square_f, square_f,
             square, vm((hid, 2 * rows), BF16), square,
@@ -498,6 +515,17 @@
         pltpu.with_memory_space_constraint(v, pltpu.HBM)
         for v in (x, we, b_enc.reshape(1, -1), wd, b_dec)
     ))
+    ge, gd = pl.pallas_call(
+        finish_kernel,
+        out_shape=(
+            jax.ShapeDtypeStruct((half * feats, hid), BF16),
+            jax.ShapeDtypeStruct((hid, total), BF16),
+        ),
+        in_specs=[in_vmem] * 3,
+        out_specs=(in_hbm, in_hbm),
+        scratch_shapes=[vm((half, feats, hid), BF16), dma((half,)), dma(())],
+        compiler_params=pltpu.CompilerParams(vmem_limit_bytes=8 * 2**20),
+    )(gp_both, xt, dec)
     return ge[None], gd[None]
 
 

time: 57 us -> 56.2 us (0.986)
  local copies, waits for them, and re-layouts: 1.83 us -> 0 us
  Pallas kernels: 54.4 us -> 55.4 us
    unnamed x2 -> x0, local copies, waits for them, and re-layouts: 1.83 us -> none
    pallas_call x0 -> x1, Pallas kernels: none -> 1.62 us  [fused_shards(): pl.pallas_call(finish_kernel, out_shape=(jax.ShapeDtypeStruct((half * fea...]
    pallas_call x1, Pallas kernels: 54.4 us -> 53.8 us  [fused_shards(): pl.pallas_call(functools.partial(kernel, n_lat, rows * 2), out_shape=(jax...]
where the time goes in v2:
time: 56.2 us; the launch traced here: 56 us
  Pallas kernels  55.4 us (99%)
  between operations  0.64 us (1%)
    pallas_call x1, Pallas kernels, fused_shards(): pl.pallas_call(functools.partial(kernel, n_lat, rows * 2), out_shape=(jax...  53.8 us
    pallas_call x1, Pallas kernels, fused_shards(): pl.pallas_call(finish_kernel, out_shape=(jax.ShapeDtypeStruct((half * fea...  1.62 us

profile of v2, /device:TPU:0, one launch (start us, length us, event | category | flops | bytes accessed | tf_op | source)
XLA Modules:
  0.0 56.0 jit_solution(13797383668007731720)
XLA Ops:
  0.6 53.8 %shard_map.68 = (bf16[384,256]{1,0:T(8,128)(2,1)S(1)}, bf16[4,384,384]{2,1,0:T(8,128)(2,1)S(1)}, bf16[256,2304]{1,0:T(8,128)(2,1)S(1)}) custom-call(bf16[192,288]{1,0:T(8,128)(2,1)} %bitcast.8, bf16[2304,256]{1,0:T(8,128)(2,1)} %bitcast.6, f32[1,256]{1,0:T(1,128)} %bitcast.9, bf16[256,2304]{1,0:T(8,128)(2,1)} %bitcast.7, bf16[1,288]{1,0:T(2,128)(2,1)} %bd_hbm.1), custom_call_target="tpu_custom_call" | custom-call | tf_op jit(solution)/shard_map/pallas_call | solution.py:483
  54.4 1.6 %shard_map.69 = (bf16[1152,256]{1,0:T(8,128)(2,1)}, bf16[256,2304]{1,0:T(8,128)(2,1)}) custom-call(bf16[384,256]{1,0:T(8,128)(2,1)S(1)} %get-tuple-element.7.gp_ref, bf16[4,384,384]{2,1,0:T(8,128)(2,1)S(1)} %get-tuple-element.8.xt_ref, bf16[256,2304]{1,0:T(8,128)(2,1)S(1)} %get-tuple-element.9.dec_ref), custom_call_target="tpu_custom_call" | custom-call | tf_op jit(solution)/shard_map/pallas_call | solution.py:518

commit v3 on v2

--- a/solution.py
+++ b/solution.py
@@ -93,6 +93,13 @@
     def cross(k):
         return 2 * peer(k) + 1 - xx
 
+    def slot(zt, side):
+        return peer(zt) + nz * ((side + xx) % 2)
+
+    def tok_slot(of, i):
+        low, high = slot(i // 2, i % 2), slot(nz // 2 + i // 2, i % 2)
+        return jnp.where(of == 0, low, high)
+
     loads = [
         pltpu.make_async_copy(src, dst, load_sem.at[i])
         for i, (src, dst) in enumerate(
@@ -101,13 +108,14 @@
     ]
     we_loads = []
     for j in range(n_lat):
-        lo = j * feats
+        lo = (same(j) if j < nz else cross(j - nz)) * feats
+        lo, after = pl.multiple_of(lo, rest), pl.multiple_of(lo + main, rest)
         we_loads.append(pltpu.make_async_copy(
             we_hbm.at[pl.ds(lo, main)], we.at[j, pl.ds(0, main)], we_sem.at[j, 0]
         ))
         for g in range(groups):
             we_loads.append(pltpu.make_async_copy(
-                we_hbm.at[pl.ds(lo + main, rest)], we.at[j, pl.ds(main + g * rest, rest)],
+                we_hbm.at[pl.ds(after, rest)], we.at[j, pl.ds(main + g * rest, rest)],
                 we_sem.at[j, 1 + g],
             ))
     loads[0].start()
@@ -156,37 +164,36 @@
         return [spread(ref[c, j]) for c in range(CHUNKS)]
 
     def gather(buf, ss, rs):
-        def send(way, c, j):
+        def send(way, c, j, to):
             where = across if way == 0 else {"latent": same(way)}
-            return remote(buf.at[c, j], buf.at[c, j], ss.at[way, c, j], rs.at[c, j], where)
+            return remote(buf.at[c, j], buf.at[c, to], ss.at[way, c, j], rs.at[c, to], where)
 
         def own(c):
-            send(0, c, lat).start()
-            send(1, c, lat).start()
-            pl.when(inner)(lambda: send(3, c, lat).start())
-            send(2, c, lat).start()
+            send(0, c, 0, nz).start()
+            send(2, c, 0, 2).start()
+            send(1, c, 0, 1).start()
+            pl.when(inner)(lambda: send(3, c, 0, 3).start())
 
         def relay(c, k):
-            j = same(k)
-            send(0, c, j).wait_recv()
-            send(0, c, j).start()
+            send(k, c, 0, k).wait_recv()
+            send(0, c, k, nz + k).start()
             if k == 2:
-                pl.when(inner)(lambda: send(1, c, j).start())
+                pl.when(inner)(lambda: send(1, c, 2, 3).start())
 
         def arrive(c, k):
-            send(0, c, cross(k)).wait_recv()
+            send(0, c, k, nz + k).wait_recv()
 
         def finish():
             for c in range(CHUNKS):
                 for k in range(nz):
-                    send(0, c, same(k)).wait_send()
-                send(1, c, lat).wait_send()
-                send(2, c, lat).wait_send()
+                    send(0, c, k, nz + k).wait_send()
+                send(1, c, 0, 1).wait_send()
+                send(2, c, 0, 2).wait_send()
 
                 @pl.when(inner)
                 def _():
-                    send(3, c, lat).wait_send()
-                    send(1, c, same(2)).wait_send()
+                    send(3, c, 0, 3).wait_send()
+                    send(1, c, 2, 3).wait_send()
 
         return own, relay, arrive, finish
 
@@ -195,7 +202,7 @@
 
     def x_tok(i):
         return remote(
-            xb.at[:, half * tok_o + i], xo.at[:, i], xo_ss.at[i], xo_rs.at[i], other_tok
+            xb.at[:, tok_slot(tok_o, i)], xo.at[:, i], xo_ss.at[i], xo_rs.at[i], other_tok
         )
 
     def g_tok(c):
@@ -243,23 +250,23 @@
         return pack(jnp.dot(act[c], wd[j], preferred_element_type=F32))
 
     def x_out(c, k):
-        xs[c, k] = decode(c, cross(k)).astype(BF16)
+        xs[c, k] = decode(c, nz + k).astype(BF16)
         x_send(c, k).start()
 
     def z_out(c, k):
-        mine = decode(c, same(k))
+        mine = decode(c, k)
         x_send(c, k).wait_recv()
         zs[c, k] = (mine + xr[c, k].astype(F32)).astype(BF16)
         z_send(c, k).start()
 
     def settle(c):
-        total = decode(c, lat) + bias_x[c]
+        total = decode(c, 0) + bias_x[c]
         x_send(c, 0).wait_recv()
         total += xr[c, 0].astype(F32)
         for k in range(1, nz):
             z_send(c, k).wait_recv()
             total += cr[c, k].astype(F32)
-        gb[c, lat] = (2.0 / tokens * total).astype(BF16)
+        gb[c, 0] = (2.0 / tokens * total).astype(BF16)
         g_own(c)
 
     def back(c, j):
@@ -270,7 +277,7 @@
 
     def back_first(c):
         pre[c] = lax.dot_general(
-            spread(gb[c, lat]), wd[lat], (((1,), (1,)), ((), ())), preferred_element_type=F32
+            spread(gb[c, 0]), wd[0], (((1,), (1,)), ((), ())), preferred_element_type=F32
         )
 
     def h_out(c):
@@ -280,8 +287,10 @@
 
     def grad_pre(c):
         h_copy(c).wait_recv()
-        gp[c] = ((pre[c] + hr[c].astype(F32)) * slope[c]).astype(BF16)
+        value = ((pre[c] + hr[c].astype(F32)) * slope[c]).astype(BF16)
+        gp[c] = value
         p_copy(c).start()
+        gp_both[c * part:(c + 1) * part] = value
 
     def both(own, other, j_own, j_other):
         return jnp.concatenate(spread_all(own, j_own) + spread_all(other, j_other), axis=0)
@@ -289,7 +298,7 @@
     def turn_x():
         for i in range(half):
             x_tok(i).wait_recv()
-            xt[i] = both(xb, xo, half * tok + i, i).T
+            xt[i] = both(xb, xo, tok_slot(tok, i), i).T
 
     def turn_act():
         for c in range(CHUNKS):
@@ -303,7 +312,7 @@
         for k in range(n_lat):
             lo = k * feats
             w_rest = wdv[:, lo + main:lo + feats]
-            wd[k] = jnp.concatenate([wdv[:, lo:lo + main]] + [w_rest] * groups, axis=1)
+            wd[slot(k // 2, k % 2)] = jnp.concatenate([wdv[:, lo:lo + main]] + [w_rest] * groups, axis=1)
 
     def fill_bias():
         bias = bd_ref[...].astype(F32)
@@ -314,13 +323,41 @@
             axis=0,
         )
         for c in range(CHUNKS):
-            bias_x[c] = block - xb[c, lat].astype(F32)
+            bias_x[c] = block - xb[c, 0].astype(F32)
+
+    def other_pre(c):
+        gp_both[rows + c * part:rows + (c + 1) * part] = gp_o[c]
+
+    def dec_grad(first, last):
+        row = []
+        for j in range(first, last):
+            at = slot(j // 2, j % 2)
+            dw = jnp.dot(act_t[...], both(gb, go, at, at), preferred_element_type=F32)
+            r = dw[:, main:main + rest]
+            for g in range(1, groups):
+                r = r + dw[:, main + g * rest:main + (g + 1) * rest]
+            row += [dw[:, :main], r]
+            if (j + 1) * feats % LANES == 0:
+                width = sum(p.shape[1] for p in row)
+                od_ref[:, (j + 1) * feats - width:(j + 1) * feats] = jnp.concatenate(
+                    row, axis=1
+                ).astype(BF16)
+                row = []
+
+    def sums_finish():
+        for c in range(CHUNKS):
+            for copy in (y_copy, a_copy):
+                copy(c).wait_send()
+            x_send(c, 0).wait_send()
+            for k in range(1, nz):
+                x_send(c, k).wait_send()
+                z_send(c, k).wait_send()
 
     x_load.wait()
     tail = x_ref[:, main:]
     wide = jnp.concatenate([x_ref[:, :main]] + [tail] * groups, axis=1).astype(F32)
     for c in range(CHUNKS):
-        xb[c, lat] = pack(wide[c * part:(c + 1) * part]).astype(BF16)
+        xb[c, 0] = pack(wide[c * part:(c + 1) * part]).astype(BF16)
 
     pl.semaphore_wait(barrier, nz + 2)
     for c in range(CHUNKS):
@@ -330,7 +367,7 @@
     be_load.wait()
     bd_load.wait()
     for c in range(CHUNKS):
-        pre[c] = jnp.dot(spread(xb[c, lat]), we[lat], preferred_element_type=F32)
+        pre[c] = jnp.dot(spread(xb[c, 0]), we[0], preferred_element_type=F32)
     widen_decoder()
     fill_bias()
 
@@ -338,12 +375,12 @@
         for k in range(1, nz):
             x_relay(c, k)
         for k in range(1, nz):
-            encode(c, same(k))
+            encode(c, k)
 
     def arrive_encode(c):
         for k in range(nz):
             x_arrive(c, k)
-            encode(c, cross(k))
+            encode(c, nz + k)
 
     relay_encode(0)
     relay_encode(1)
@@ -374,6 +411,9 @@
     for k in (3, 2, 1):
         z_out(2, k)
     turn_act()
+    x_finish()
+    for i in range(half):
+        x_tok(i).wait_send()
     settle(1)
     back_first(0)
 
@@ -381,12 +421,12 @@
         for k in range(1, nz):
             g_relay(c, k)
         for k in range(1, nz):
-            back(c, same(k))
+            back(c, k)
 
     def arrive_back(c):
         for k in range(nz):
             g_arrive(c, k)
-            back(c, cross(k))
+            back(c, nz + k)
 
     relay_back(0)
     settle(2)
@@ -399,45 +439,24 @@
     arrive_back(1)
     h_out(1)
     grad_pre(0)
+    sums_finish()
     arrive_back(2)
     h_out(2)
     grad_pre(1)
+    p_copy(0).wait_recv()
+    other_pre(0)
     for c in range(CHUNKS):
         g_tok(c).wait_recv()
-
-    row = []
-    for j in range(n_lat):
-        dw = jnp.dot(act_t[...], both(gb, go, j, j), preferred_element_type=F32)
-        r = dw[:, main:main + rest]
-        for g in range(1, groups):
-            r = r + dw[:, main + g * rest:main + (g + 1) * rest]
-        row += [dw[:, :main], r]
-        if (j + 1) * feats % LANES == 0:
-            width = sum(p.shape[1] for p in row)
-            od_ref[:, (j + 1) * feats - width:(j + 1) * feats] = jnp.concatenate(
-                row, axis=1
-            ).astype(BF16)
-            row = []
-
+    dec_grad(0, half)
     grad_pre(2)
+    g_finish()
+    dec_grad(half, n_lat)
     for c in range(CHUNKS):
+        for copy in (g_tok, h_copy, p_copy):
+            copy(c).wait_send()
+    for c in range(1, CHUNKS):
         p_copy(c).wait_recv()
-    half_rows = CHUNKS * part
-    for c in range(CHUNKS):
-        gp_both[c * part:(c + 1) * part] = gp[c]
-        gp_both[half_rows + c * part:half_rows + (c + 1) * part] = gp_o[c]
-
-    x_finish()
-    g_finish()
-    for i in range(half):
-        x_tok(i).wait_send()
-    for c in range(CHUNKS):
-        for copy in (g_tok, y_copy, a_copy, h_copy, p_copy):
-            copy(c).wait_send()
-        x_send(c, 0).wait_send()
-        for k in range(1, nz):
-            x_send(c, k).wait_send()
-            z_send(c, k).wait_send()
+        other_pre(c)
 
 
 def finish_kernel(gp_ref, xt_ref, dec_ref, oe_hbm, od_hbm, oe, sem, dec_sem):

time: 56.2 us -> 55.3 us (0.984)
  Pallas kernels: 55.4 us -> 54.5 us
    pallas_call x1, Pallas kernels: 53.8 us -> 52.9 us  [fused_shards(): pl.pallas_call(functools.partial(kernel, n_lat, rows * 2), out_shape=(jax...]
where the time goes in v3:
time: 55.3 us; the launch traced here: 55.1 us
  Pallas kernels  54.5 us (99%)
  between operations  0.64 us (1%)
    pallas_call x1, Pallas kernels, fused_shards(): pl.pallas_call(functools.partial(kernel, n_lat, rows * 2), out_shape=(jax...  52.9 us
    pallas_call x1, Pallas kernels, fused_shards(): pl.pallas_call(finish_kernel, out_shape=(jax.ShapeDtypeStruct((half * fea...  1.63 us

profile of v3, /device:TPU:0, one launch (start us, length us, event | category | flops | bytes accessed | tf_op | source)
XLA Modules:
  0.0 55.1 jit_solution(14564066739362675139)
XLA Ops:
  0.6 52.9 %shard_map.68 = (bf16[384,256]{1,0:T(8,128)(2,1)S(1)}, bf16[4,384,384]{2,1,0:T(8,128)(2,1)S(1)}, bf16[256,2304]{1,0:T(8,128)(2,1)S(1)}) custom-call(bf16[192,288]{1,0:T(8,128)(2,1)} %bitcast.8, bf16[2304,256]{1,0:T(8,128)(2,1)} %bitcast.6, f32[1,256]{1,0:T(1,128)} %bitcast.9, bf16[256,2304]{1,0:T(8,128)(2,1)} %bitcast.7, bf16[1,288]{1,0:T(2,128)(2,1)} %bd_hbm.1), custom_call_target="tpu_custom_call" | custom-call | tf_op jit(solution)/shard_map/pallas_call | solution.py:502
  53.5 1.6 %shard_map.69 = (bf16[1152,256]{1,0:T(8,128)(2,1)}, bf16[256,2304]{1,0:T(8,128)(2,1)}) custom-call(bf16[384,256]{1,0:T(8,128)(2,1)S(1)} %get-tuple-element.7.gp_ref, bf16[4,384,384]{2,1,0:T(8,128)(2,1)S(1)} %get-tuple-element.8.xt_ref, bf16[256,2304]{1,0:T(8,128)(2,1)S(1)} %get-tuple-element.9.dec_ref), custom_call_target="tpu_custom_call" | custom-call | tf_op jit(solution)/shard_map/pallas_call | solution.py:537
